TPU v7x, 32 devices: a whole 2x2x4 slice. The times are simulated.
32 devices in a mesh: row: 4 (over y, core), col: 8 (over z, x).
Axes of the slice: x: 2, y: 2, z: 4, core: 2. Of those that a mesh axis runs over, the one named last changes fastest.
Arguments:
- inverse: float32 [16384, 16384], P('row', 'col'), may hold values from -6 to 6
- front_blocks: int32 [2, 16], replicated, may hold values from 0 to 63, as said below
- panels: float32 [2, 4096, 256], P(None, 'row'), may hold values from -0.09375 to 0.09375
- diag_terms: float32 [2, 256, 256], replicated, may hold values from -6 to 6
- bounds: int32 [2, 4], replicated, may hold values from 1 to 128, 256 in all within a row
Outputs:
- border: float32 [2, 4096, 256], P(None, ('row', 'col'))
- diag_block: float32 [2, 256, 256], replicated
Inputs may be any that keep to these rules, and one draw needn't show every extreme that they name: `front_blocks`: each row names 16 distinct blocks. Positions 4 r to 4 r + 3 name blocks of four different groups of 16 consecutive blocks, and every such group is named at exactly four positions, of four different r. Positions 2 o and 2 o + 1 name blocks of two different groups of 8 consecutive blocks, and every such group is named at exactly two positions, of two different o.
All inputs are finite; a program needn't handle non-finite values.
Results may differ from a plain program's by a relative error of at most 0.0001.
Values sent between devices are 32-bit elements; how exact they have to be, the bound alone decides.
A program may use at most 128 MiB of HBM per device.

v0:
```python
import jax
import jax.numpy as jnp
from jax import lax
from jax.sharding import PartitionSpec as P

BS = 256


def body(inverse, front_blocks, panels, diag_terms, bounds):
    n_row = lax.axis_size("row")
    n_col = lax.axis_size("col")
    row_index = lax.axis_index("row")
    col_index = lax.axis_index("col")
    rows_loc, cols_loc = inverse.shape
    row_group = rows_loc // BS
    col_group = cols_loc // BS
    list_length = front_blocks.shape[1]
    per_owner = list_length // n_row
    highest = lax.Precision.HIGHEST
    borders = []
    diagonals = []
    for front_index in range(2):
        front_list = front_blocks[front_index]
        own_blocks = lax.dynamic_slice_in_dim(front_list, row_index * per_owner, per_owner)
        w_loc = panels[front_index]
        panel_width = w_loc.shape[1]
        w_pieces = w_loc.reshape(per_owner, BS, panel_width)
        targets = col_index * col_group + jnp.arange(col_group, dtype=jnp.int32)
        picker = (own_blocks[None, :] == targets[:, None]).astype(jnp.float32)
        own_piece = jnp.einsum("ki,iab->ab", picker, w_pieces, precision=highest)
        slot_rows = lax.all_gather(own_piece, "row", axis=0, tiled=True).reshape(
            n_row, BS, panel_width
        )
        owners = front_list.reshape(n_row, per_owner)
        placer = jnp.sum((owners[None, :, :] == targets[:, None, None]).astype(jnp.float32), axis=2)
        w_tilde = jnp.einsum("ks,sab->kab", placer, slot_rows, precision=highest).reshape(
            cols_loc, panel_width
        )
        dest_lists = front_list.reshape(n_row, per_owner)
        local_ids = row_index * row_group + jnp.arange(row_group, dtype=jnp.int32)
        share_rows = per_owner * BS // n_col
        full_rows = jnp.dot(inverse, w_tilde, precision=highest)
        quarters = BS // share_rows
        full_pieces = full_rows.reshape(row_group, quarters, share_rows, panel_width)
        first_rows = jnp.arange(n_col, dtype=jnp.int32) * share_rows
        dest_block = dest_lists[:, first_rows // BS]
        block_pick = (dest_block.T[:, :, None] == local_ids[None, None, :]).astype(jnp.float32)
        quarter_pick = (
            (first_rows % BS // share_rows)[:, None]
            == jnp.arange(quarters, dtype=jnp.int32)[None, :]
        ).astype(jnp.float32)
        sectioned = jnp.einsum("cq,kqap->ckap", quarter_pick, full_pieces, precision=highest)
        ordered = jnp.einsum("cdk,ckap->cdap", block_pick, sectioned, precision=highest)
        ordered = ordered.reshape(n_col * n_row * share_rows, panel_width)
        reduced = lax.psum_scatter(ordered, "col", scatter_dimension=0, tiled=True)
        received = lax.all_to_all(
            reduced.reshape(n_row, share_rows, panel_width),
            "row",
            split_axis=0,
            concat_axis=0,
            tiled=True,
        )
        product = jnp.sum(received, axis=0)
        w_mine = lax.dynamic_slice_in_dim(w_loc, col_index * share_rows, share_rows, 0)
        own_term = jnp.dot(w_mine.T, product, precision=highest)
        summed_total = lax.psum(own_term, ("row", "col"))
        node_ends = jnp.cumsum(bounds[front_index])
        columns = jnp.arange(panel_width, dtype=jnp.int32)
        node_ids = jnp.sum((columns[:, None] >= node_ends[None, :]).astype(jnp.int32), axis=1)
        same_node = (node_ids[:, None] == node_ids[None, :]).astype(jnp.float32)
        borders.append(-product)
        diagonals.append(same_node * (diag_terms[front_index] + summed_total))
    return (jnp.stack(borders), jnp.stack(diagonals))


def solution(mesh):
    placed = (P("row", "col"), P(), P(None, "row", None), P(), P())
    return jax.shard_map(
        body,
        mesh=mesh,
        in_specs=placed,
        out_specs=(P(None, ("row", "col"), None), P()),
        check_vma=False,
    )
```

profile of v0, /device:TPU:0, one launch (start us, length us, event | category | flops | bytes accessed | tf_op | source)
XLA Modules:
  0.0 484.4 jit_solution(6554460476007873666)
XLA Ops:
  8.0 1.7 fusion.46
  10.0 2.3 fusion.6
  13.1 2.3 fusion.4
  17.2 15.4 %all-gather.3.cloned.1.call-done = f32[1024,256]{1,0:T(8,128)} async-done(((f32[256,256]{1,0:T(8,128)}), f32[1024,256]{1,0:T(8,128)}) %all-gather.3.cloned.1.call-update) | async-done | bytes 1048592 | tf_op jit(solution)/shard_map/all_gather | solution.py:31
  32.6 4.0 fusion.10
  37.4 58.5 %convolution_bitcast_fusion.1 = f32[4096,256]{0,1:T(8,128)} fusion(f32[2048,256]{1,0:T(8,128)S(1)} %bitcast.104, f32[4096,2048]{1,0:T(8,128)} %param.5), kind=kOutput, calls=%fused_computation.7 | convolution fusion | flops 25769803776 | bytes 39845888 | tf_op jit(solution)/shard_map/dot_general | solution.py:42
  95.9 6.6 %reshape.215 = f32[16,2,128,256]{2,1,0,3:T(2,128)} reshape(f32[4096,256]{0,1:T(8,128)} %convolution_bitcast_fusion.1) | data formatting | bytes 8388608 | tf_op jit(solution)/shard_map/reshape | solution.py:44
  102.5 9.3 %copy.20 = f32[16,2,128,256]{3,1,2,0:T(2,128)} copy(f32[16,2,128,256]{2,1,0,3:T(2,128)} %reshape.215) | data formatting | bytes 8388608 | tf_op jit(solution)/shard_map/reshape | solution.py:44
  111.8 11.7 %fusion.34 = f32[8,16,128,256]{3,0,2,1:T(8,128)S(1)} fusion(f32[16,2,128,256]{3,1,2,0:T(2,128)} %copy.20, s32[8]{0:T(128)S(1)} %and_select_fusion), kind=kOutput, calls=%fused_computation.58 | convolution fusion | flops 100663312 | bytes 20971552 | tf_op jit(solution)/shard_map/cq,kqap->ckap/dot_general | solution.py:52
  123.5 12.2 %fusion.2 = f32[8,4,128,256]{3,1,2,0:T(4,128)S(1)} fusion(f32[8,16,128,256]{3,0,2,1:T(8,128)S(1)} %fusion.34, s32[16]{0:T(128)S(1)} %iota_add_fusion.1, s32[8,4]{1,0:T(8,128)S(1)} %gather_fusion), kind=kOutput, calls=%fused_computation.4 | convolution fusion | flops 201327104 | bytes 20971712 | tf_op jit(solution)/shard_map/cdk,ckap->cdap/dot_general | solution.py:53
  135.7 2.7 copy.22
  139.1 4.0 fusion.8
  143.8 58.8 %convolution_bitcast_fusion = f32[4096,256]{0,1:T(8,128)} fusion(f32[2048,256]{1,0:T(8,128)S(1)} %bitcast.105, f32[4096,2048]{1,0:T(8,128)} %param.5), kind=kOutput, calls=%fused_computation.6 | convolution fusion | flops 25769803776 | bytes 39845888 | tf_op jit(solution)/shard_map/dot_general | solution.py:42
  202.6 6.7 %reshape.220 = f32[16,2,128,256]{2,1,0,3:T(2,128)} reshape(f32[4096,256]{0,1:T(8,128)} %convolution_bitcast_fusion) | data formatting | bytes 8388608 | tf_op jit(solution)/shard_map/reshape | solution.py:44
  209.3 9.3 %copy.26 = f32[16,2,128,256]{3,1,2,0:T(2,128)} copy(f32[16,2,128,256]{2,1,0,3:T(2,128)} %reshape.220) | data formatting | bytes 8388608 | tf_op jit(solution)/shard_map/reshape | solution.py:44
  218.6 11.7 %fusion.32 = f32[8,16,128,256]{3,0,2,1:T(8,128)S(1)} fusion(f32[16,2,128,256]{3,1,2,0:T(2,128)} %copy.26, s32[8]{0:T(128)S(1)} %and_select_fusion), kind=kOutput, calls=%fused_computation.56 | convolution fusion | flops 100663312 | bytes 20971552 | tf_op jit(solution)/shard_map/cq,kqap->ckap/dot_general | solution.py:52
  230.3 12.2 %fusion = f32[8,4,128,256]{3,1,2,0:T(4,128)S(1)} fusion(f32[8,16,128,256]{3,0,2,1:T(8,128)S(1)} %fusion.32, s32[8,4]{1,0:T(8,128)S(1)} %gather_fusion.1, s32[16]{0:T(128)S(1)} %iota_add_fusion.1), kind=kOutput, calls=%fused_computation.2 | convolution fusion | flops 201327104 | bytes 20971712 | tf_op jit(solution)/shard_map/cdk,ckap->cdap/dot_general | solution.py:53
  242.5 2.7 copy.28
  245.3 3.6 all-to-all-start
  249.4 84.5 %reduce-scatter.5.cloned.1.call-done = f32[512,256]{1,0:T(8,128)} async-done(((f32[4096,256]{1,0:T(8,128)}), f32[512,256]{1,0:T(8,128)}) %reduce-scatter.5.cloned.1.call-update) | async-done | bytes 524304 | tf_op jit(solution)/shard_map/reduce_scatter | solution.py:55
  333.9 3.5 all-to-all-start.1
  337.5 2.1 fusion.18
  339.5 6.6 %all-to-all-done.1 = f32[4,128,256]{2,1,0:T(8,128)S(1)} async-done(((f32[4,128,256]{2,1,0:T(8,128)}), f32[4,128,256]{2,1,0:T(8,128)S(1)}, u32[]{:S(2)}, u32[]{:S(2)}) %all-to-all-start.1) | async-done | bytes 524320 | tf_op jit(solution)/shard_map/all_to_all | solution.py:56
  348.1 127.4 %all-reduce.3.cloned.1.call-done = (f32[256,256]{1,0:T(8,128)}, f32[256,256]{1,0:T(8,128)}) async-done(((f32[256,256]{1,0:T(8,128)}, f32[256,256]{1,0:T(8,128)}), (f32[256,256]{1,0:T(8,128)}, f32[256,256]{1,0:T(8,128)})) %all-reduce.3.cloned.1.call-update) | async-done | bytes 524304 | tf_op jit(solution)/shard_map/psum | solution.py:66
  (50 shorter events, 10.2 us)
Async XLA Ops:
  7.2 25.5 %all-gather.3.cloned.1.call-start = ((), (), s32[]{:S(2)}) async-start(), calls=%async_computation.4 | async-start | bytes 1310720 | tf_op jit(solution)/shard_map/all_gather | solution.py:31
  9.7 27.7 %copy-start = (f32[1,1024,256]{2,1,0:T(8,128)}, f32[1,1024,256]{2,1,0:T(8,128)S(1)}, u32[]{:S(2)}) copy-start(f32[1,1024,256]{2,1,0:T(8,128)S(1)} %get-tuple-element.10) | copy-start | bytes 3145732
  13.1 126.1 %all-gather.5.cloned.1.call-start = ((), (), s32[]{:S(2)}) async-start(), calls=%async_computation.6 | async-start | bytes 1310720 | tf_op jit(solution)/shard_map/all_gather | solution.py:31
  16.2 229.1 %reduce-scatter.3.cloned.1.call-start = ((), (), s32[]{:S(2)}) async-start(), calls=%async_computation.5 | async-start | bytes 4718592 | tf_op jit(solution)/shard_map/reduce_scatter | solution.py:55
  138.4 195.5 %reduce-scatter.5.cloned.1.call-start = ((), (), s32[]{:S(2)}) async-start(), calls=%async_computation.7 | async-start | bytes 4718592 | tf_op jit(solution)/shard_map/reduce_scatter | solution.py:55
  245.2 3.7 copy-start.2
  245.2 230.3 %copy-start.1 = (f32[2,256,256]{2,1,0:T(8,128)S(1)}, f32[2,256,256]{2,1,0:T(8,128)}, u32[]{:S(2)}) copy-start(f32[2,256,256]{2,1,0:T(8,128)} %param.8) | copy-start | bytes 1572868
  245.3 88.6 %all-to-all-start = ((f32[4,128,256]{2,1,0:T(8,128)}), f32[4,128,256]{2,1,0:T(8,128)S(1)}, u32[]{:S(2)}, u32[]{:S(2)}) async-start(f32[4,128,256]{2,1,0:T(8,128)} %bitcast.112), calls=%async_computation.1 | async-start | bytes 1048576 | tf_op jit(solution)/shard_map/all_to_all | solution.py:56
  333.9 12.3 %all-to-all-start.1 = ((f32[4,128,256]{2,1,0:T(8,128)}), f32[4,128,256]{2,1,0:T(8,128)S(1)}, u32[]{:S(2)}, u32[]{:S(2)}) async-start(f32[4,128,256]{2,1,0:T(8,128)} %bitcast.113), calls=%async_computation.3 | async-start | bytes 1048576 | tf_op jit(solution)/shard_map/all_to_all | solution.py:56
  337.3 138.2 %all-reduce.3.cloned.1.call-start = ((), (), s32[]{:S(2)}) async-start(), calls=%async_computation.8 | async-start | bytes 1048576 | tf_op jit(solution)/shard_map/psum | solution.py:66
Sparse Core Ops, SparseCore 0:
  13.2 19.4 all-gather.2
  34.8 16.6 all-gather.4
  138.5 88.2 reduce-scatter.2
  245.4 88.4 reduce-scatter.4
  347.4 128.0 all-reduce.2
where the time goes:
time: 492 us; the launch traced here: 484 us
  waiting for transfers between devices  234 us (48%)
  matrix products  181 us (37%)
  local copies, waits for them, and re-layouts  44.1 us (9%)
  between operations  14.4 us (3%)
  starting transfers between devices  7.29 us (1%)
    psum x1, waiting for transfers between devices, body(): summed_total = lax.psum(own_term, ('row', 'col'))  127 us
    dot_general x2, matrix products, body(): full_rows = jnp.dot(inverse, w_tilde, precision=highest)  117 us
    reduce_scatter x2, waiting for transfers between devices, body(): reduced = lax.psum_scatter(ordered, 'col', scatter_dimension=0, tiled=True)  84.5 us
    reshape x4, local copies, waits for them, and re-layouts, body(): full_rows.reshape(row_group, quarters, share_rows, panel_width)  31.9 us
    dot_general x2, matrix products, body(): jnp.einsum('cdk,ckap->cdap', block_pick, sectioned, precision=highest)  24.4 us
    dot_general x2, matrix products, body(): jnp.einsum('cq,kqap->ckap', quarter_pick, full_pieces, precision=highest)  23.4 us
    all_gather x2, waiting for transfers between devices, body(): lax.all_gather(own_piece, 'row', axis=0, tiled=True)  15.4 us
  transfers between devices with their start and end apart: 7, of which 4 were waited for; matrix products, arithmetic and copies ran while one was open for 45% of the time, Pallas kernels for 0%

commit v1 on v0

--- a/solution.py
+++ b/solution.py
@@ -63,7 +63,9 @@
         product = jnp.sum(received, axis=0)
         w_mine = lax.dynamic_slice_in_dim(w_loc, col_index * share_rows, share_rows, 0)
         own_term = jnp.dot(w_mine.T, product, precision=highest)
-        summed_total = lax.psum(own_term, ("row", "col"))
+        summed_total = own_term
+        for i in ("row", "col"):
+            summed_total = lax.psum(summed_total, i)
         node_ends = jnp.cumsum(bounds[front_index])
         columns = jnp.arange(panel_width, dtype=jnp.int32)
         node_ids = jnp.sum((columns[:, None] >= node_ends[None, :]).astype(jnp.int32), axis=1)

time: 492 us -> 473 us (0.961)
  waiting for transfers between devices: 234 us -> 214 us
    psum x1 -> x2, waiting for transfers between devices: 127 us -> 107 us  [body(): summed_total = lax.psum(summed_total, i)]
  transfers between devices with their start and end apart: 7 -> 8, of which waited for: 4 -> 5; matrix products, arithmetic and copies ran while one was open for 45% -> 47% of each run, Pallas kernels for 0% -> 0%
where the time goes in v1:
time: 473 us; the launch traced here: 465 us
  waiting for transfers between devices  214 us (45%)
  matrix products  181 us (38%)
  local copies, waits for them, and re-layouts  44.1 us (9%)
  between operations  14.7 us (3%)
  starting transfers between devices  7.33 us (2%)
    dot_general x2, matrix products, body(): full_rows = jnp.dot(inverse, w_tilde, precision=highest)  117 us
    psum x2, waiting for transfers between devices, body(): summed_total = lax.psum(summed_total, i)  107 us
    reduce_scatter x2, waiting for transfers between devices, body(): reduced = lax.psum_scatter(ordered, 'col', scatter_dimension=0, tiled=True)  85 us
    reshape x4, local copies, waits for them, and re-layouts, body(): full_rows.reshape(row_group, quarters, share_rows, panel_width)  31.9 us
    dot_general x2, matrix products, body(): jnp.einsum('cdk,ckap->cdap', block_pick, sectioned, precision=highest)  24.4 us
    dot_general x2, matrix products, body(): jnp.einsum('cq,kqap->ckap', quarter_pick, full_pieces, precision=highest)  23.4 us
    all_gather x2, waiting for transfers between devices, body(): lax.all_gather(own_piece, 'row', axis=0, tiled=True)  15.4 us
  transfers between devices with their start and end apart: 8, of which 5 were waited for; matrix products, arithmetic and copies ran while one was open for 47% of the time, Pallas kernels for 0%

profile of v1, /device:TPU:0, one launch (start us, length us, event | category | flops | bytes accessed | tf_op | source)
XLA Modules:
  0.0 465.2 jit_solution(10666742543191495199)
XLA Ops:
  10.0 2.3 fusion.6
  13.1 2.3 fusion.4
  17.2 15.4 %all-gather.3.cloned.1.call-done = f32[1024,256]{1,0:T(8,128)} async-done(((f32[256,256]{1,0:T(8,128)}), f32[1024,256]{1,0:T(8,128)}) %all-gather.3.cloned.1.call-update) | async-done | bytes 1048592 | tf_op jit(solution)/shard_map/all_gather | solution.py:31
  32.6 4.0 fusion.10
  37.4 58.5 %convolution_bitcast_fusion.1 = f32[4096,256]{0,1:T(8,128)} fusion(f32[2048,256]{1,0:T(8,128)S(1)} %bitcast.104, f32[4096,2048]{1,0:T(8,128)} %param.5), kind=kOutput, calls=%fused_computation.7 | convolution fusion | flops 25769803776 | bytes 39845888 | tf_op jit(solution)/shard_map/dot_general | solution.py:42
  95.9 6.6 %reshape.215 = f32[16,2,128,256]{2,1,0,3:T(2,128)} reshape(f32[4096,256]{0,1:T(8,128)} %convolution_bitcast_fusion.1) | data formatting | bytes 8388608 | tf_op jit(solution)/shard_map/reshape | solution.py:44
  102.5 9.3 %copy.20 = f32[16,2,128,256]{3,1,2,0:T(2,128)} copy(f32[16,2,128,256]{2,1,0,3:T(2,128)} %reshape.215) | data formatting | bytes 8388608 | tf_op jit(solution)/shard_map/reshape | solution.py:44
  111.8 11.7 %fusion.34 = f32[8,16,128,256]{3,0,2,1:T(8,128)S(1)} fusion(f32[16,2,128,256]{3,1,2,0:T(2,128)} %copy.20, s32[8]{0:T(128)S(1)} %and_select_fusion), kind=kOutput, calls=%fused_computation.58 | convolution fusion | flops 100663312 | bytes 20971552 | tf_op jit(solution)/shard_map/cq,kqap->ckap/dot_general | solution.py:52
  123.5 12.2 %fusion.2 = f32[8,4,128,256]{3,1,2,0:T(4,128)S(1)} fusion(f32[8,16,128,256]{3,0,2,1:T(8,128)S(1)} %fusion.34, s32[16]{0:T(128)S(1)} %iota_add_fusion.1, s32[8,4]{1,0:T(8,128)S(1)} %gather_fusion), kind=kOutput, calls=%fused_computation.4 | convolution fusion | flops 201327104 | bytes 20971712 | tf_op jit(solution)/shard_map/cdk,ckap->cdap/dot_general | solution.py:53
  135.7 2.7 copy.22
  139.1 4.0 fusion.8
  143.8 58.8 %convolution_bitcast_fusion = f32[4096,256]{0,1:T(8,128)} fusion(f32[2048,256]{1,0:T(8,128)S(1)} %bitcast.105, f32[4096,2048]{1,0:T(8,128)} %param.5), kind=kOutput, calls=%fused_computation.6 | convolution fusion | flops 25769803776 | bytes 39845888 | tf_op jit(solution)/shard_map/dot_general | solution.py:42
  202.6 6.7 %reshape.220 = f32[16,2,128,256]{2,1,0,3:T(2,128)} reshape(f32[4096,256]{0,1:T(8,128)} %convolution_bitcast_fusion) | data formatting | bytes 8388608 | tf_op jit(solution)/shard_map/reshape | solution.py:44
  209.3 9.3 %copy.26 = f32[16,2,128,256]{3,1,2,0:T(2,128)} copy(f32[16,2,128,256]{2,1,0,3:T(2,128)} %reshape.220) | data formatting | bytes 8388608 | tf_op jit(solution)/shard_map/reshape | solution.py:44
  218.6 11.7 %fusion.32 = f32[8,16,128,256]{3,0,2,1:T(8,128)S(1)} fusion(f32[16,2,128,256]{3,1,2,0:T(2,128)} %copy.26, s32[8]{0:T(128)S(1)} %and_select_fusion), kind=kOutput, calls=%fused_computation.56 | convolution fusion | flops 100663312 | bytes 20971552 | tf_op jit(solution)/shard_map/cq,kqap->ckap/dot_general | solution.py:52
  230.3 12.2 %fusion = f32[8,4,128,256]{3,1,2,0:T(4,128)S(1)} fusion(f32[8,16,128,256]{3,0,2,1:T(8,128)S(1)} %fusion.32, s32[8,4]{1,0:T(8,128)S(1)} %gather_fusion.1, s32[16]{0:T(128)S(1)} %iota_add_fusion.1), kind=kOutput, calls=%fused_computation.2 | convolution fusion | flops 201327104 | bytes 20971712 | tf_op jit(solution)/shard_map/cdk,ckap->cdap/dot_general | solution.py:53
  242.5 2.7 copy.28
  245.3 3.6 all-to-all-start
  248.9 84.9 %reduce-scatter.5.cloned.1.call-done = f32[512,256]{1,0:T(8,128)} async-done(((f32[4096,256]{1,0:T(8,128)}), f32[512,256]{1,0:T(8,128)}) %reduce-scatter.5.cloned.1.call-update) | async-done | bytes 524304 | tf_op jit(solution)/shard_map/reduce_scatter | solution.py:55
  333.9 3.5 all-to-all-start.1
  337.4 2.0 fusion.18
  339.5 6.7 %all-to-all-done.1 = f32[4,128,256]{2,1,0:T(8,128)S(1)} async-done(((f32[4,128,256]{2,1,0:T(8,128)}), f32[4,128,256]{2,1,0:T(8,128)S(1)}, u32[]{:S(2)}, u32[]{:S(2)}) %all-to-all-start.1) | async-done | bytes 524320 | tf_op jit(solution)/shard_map/all_to_all | solution.py:56
  347.8 31.9 %all-reduce.7.cloned.1.call-done = (f32[256,256]{1,0:T(8,128)}, f32[256,256]{1,0:T(8,128)}) async-done(((f32[256,256]{1,0:T(8,128)}, f32[256,256]{1,0:T(8,128)}), (f32[256,256]{1,0:T(8,128)}, f32[256,256]{1,0:T(8,128)})) %all-reduce.7.cloned.1.call-update) | async-done | bytes 524304 | tf_op jit(solution)/shard_map/psum | solution.py:68
  380.5 75.4 %all-reduce.5.cloned.1.call-done = (f32[256,256]{1,0:T(8,128)}, f32[256,256]{1,0:T(8,128)}) async-done(((f32[256,256]{1,0:T(8,128)}, f32[256,256]{1,0:T(8,128)}), (f32[256,256]{1,0:T(8,128)}, f32[256,256]{1,0:T(8,128)})) %all-reduce.5.cloned.1.call-update) | async-done | bytes 524304 | tf_op jit(solution)/shard_map/psum | solution.py:68
  (53 shorter events, 11.9 us)
Async XLA Ops:
  7.2 25.5 %all-gather.3.cloned.1.call-start = ((), (), s32[]{:S(2)}) async-start(), calls=%async_computation.4 | async-start | bytes 1310720 | tf_op jit(solution)/shard_map/all_gather | solution.py:31
  9.7 27.7 %copy-start = (f32[1,1024,256]{2,1,0:T(8,128)}, f32[1,1024,256]{2,1,0:T(8,128)S(1)}, u32[]{:S(2)}) copy-start(f32[1,1024,256]{2,1,0:T(8,128)S(1)} %get-tuple-element.12) | copy-start | bytes 3145732
  13.1 126.1 %all-gather.5.cloned.1.call-start = ((), (), s32[]{:S(2)}) async-start(), calls=%async_computation.6 | async-start | bytes 1310720 | tf_op jit(solution)/shard_map/all_gather | solution.py:31
  16.2 229.1 %reduce-scatter.3.cloned.1.call-start = ((), (), s32[]{:S(2)}) async-start(), calls=%async_computation.5 | async-start | bytes 4718592 | tf_op jit(solution)/shard_map/reduce_scatter | solution.py:55
  138.4 195.5 %reduce-scatter.5.cloned.1.call-start = ((), (), s32[]{:S(2)}) async-start(), calls=%async_computation.7 | async-start | bytes 4718592 | tf_op jit(solution)/shard_map/reduce_scatter | solution.py:55
  245.2 102.1 %copy-start.2 = (s32[2,4]{1,0:T(2,128)S(1)}, s32[2,4]{1,0:T(2,128)}, u32[]{:S(2)}) copy-start(s32[2,4]{1,0:T(2,128)} %param.9) | copy-start | bytes 100
  245.3 210.7 %copy-start.1 = (f32[2,256,256]{2,1,0:T(8,128)S(1)}, f32[2,256,256]{2,1,0:T(8,128)}, u32[]{:S(2)}) copy-start(f32[2,256,256]{2,1,0:T(8,128)} %param.8) | copy-start | bytes 1572868
  245.3 88.6 %all-to-all-start = ((f32[4,128,256]{2,1,0:T(8,128)}), f32[4,128,256]{2,1,0:T(8,128)S(1)}, u32[]{:S(2)}, u32[]{:S(2)}) async-start(f32[4,128,256]{2,1,0:T(8,128)} %bitcast.112), calls=%async_computation.1 | async-start | bytes 1048576 | tf_op jit(solution)/shard_map/all_to_all | solution.py:56
  333.9 12.3 %all-to-all-start.1 = ((f32[4,128,256]{2,1,0:T(8,128)}), f32[4,128,256]{2,1,0:T(8,128)S(1)}, u32[]{:S(2)}, u32[]{:S(2)}) async-start(f32[4,128,256]{2,1,0:T(8,128)} %bitcast.113), calls=%async_computation.3 | async-start | bytes 1048576 | tf_op jit(solution)/shard_map/all_to_all | solution.py:56
  337.3 42.4 %all-reduce.7.cloned.1.call-start = ((), (), s32[]{:S(2)}) async-start(), calls=%async_computation.9 | async-start | bytes 1048576 | tf_op jit(solution)/shard_map/psum | solution.py:68
  347.3 108.6 %all-reduce.5.cloned.1.call-start = ((), (), s32[]{:S(2)}) async-start(), calls=%async_computation.8 | async-start | bytes 1048576 | tf_op jit(solution)/shard_map/psum | solution.py:68
Sparse Core Ops, SparseCore 0:
  13.2 19.4 all-gather.2
  34.8 16.6 all-gather.4
  138.5 88.2 reduce-scatter.2
  245.4 88.4 reduce-scatter.4
  347.4 32.2 all-reduce.6
  383.0 72.8 all-reduce.4
